TPU v7x, 32 devices: a whole 2x2x4 slice. The times are simulated.
32 devices in a mesh: blk: 8 (over y, x, core), rows: 4 (over z).
Axes of the slice: x: 2, y: 2, z: 4, core: 2. Of those that a mesh axis runs over, the one named last changes fastest.
Arguments:
- cholesky: bfloat16 [4096, 256, 256], P('blk', 'rows'), may hold values from -0.01171875 to 0.01171875
- green: bfloat16 [256, 256, 256], P('blk', 'rows'), may hold values from -18 to 18
- aux_field: float32 [256, 4096], P(None, 'blk'), may hold values from -6 to 6
- walker_orbitals: bfloat16 [256, 256, 128], P('blk', 'rows'), may hold values from -6 to 6
Outputs:
- new_orbitals: float32 [256, 256, 128], P('blk', 'rows')
- force_bias: float32 [256, 4096], P(None, 'blk')
All inputs are finite; a program needn't handle non-finite values.
Results may differ from a plain program's by a relative error of at most 0.025.
Values may be sent and summed in bfloat16 or wider, within the bound.
No kernel may reach another device: no remote copies, remote signals or barrier semaphores. Data moves between devices by JAX's collectives and lax.ppermute only.
A program may use at most 128 MiB of HBM per device.

v0:
```python
import jax
import jax.numpy as jnp
from jax import lax
from jax.sharding import PartitionSpec as P

TAYLOR = 4
time_root = 0.5


def shards(cholesky, green, aux_field, walker_orbitals):
    ch_dev, rows_dev, orbitals = cholesky.shape
    flat_chol = cholesky.reshape(ch_dev, rows_dev * orbitals)
    walk_count = walker_orbitals.shape[0]
    batch_piece = lax.all_gather(green, "blk", axis=0, tiled=True)
    flat_piece = batch_piece.reshape(batch_piece.shape[0], rows_dev * orbitals)
    partial_bias = lax.dot_general(
        flat_piece, flat_chol, (((1,), (1,)), ((), ())), preferred_element_type=jnp.float32
    )
    force_bias = lax.psum(partial_bias.astype(jnp.bfloat16), "rows").astype(jnp.float32)
    shifted = (time_root * (aux_field - force_bias)).astype(jnp.bfloat16)
    summed = lax.psum_scatter(
        jnp.dot(shifted, flat_chol, preferred_element_type=jnp.float32).astype(jnp.bfloat16),
        "blk",
        scatter_dimension=0,
        tiled=True,
    )
    potential = summed.reshape(walk_count, rows_dev, orbitals)
    result = walker_orbitals.astype(jnp.float32)
    full_potential = lax.all_gather(potential, "rows", axis=1, tiled=True)
    full_term = lax.all_gather(walker_orbitals, "rows", axis=1, tiled=True)
    offset = lax.axis_index("rows") * rows_dev
    for degree in range(1, TAYLOR + 1):
        product = jnp.einsum(
            "wik,wka->wia", full_potential, full_term, preferred_element_type=jnp.float32
        )
        full_term = (product / degree).astype(jnp.bfloat16)
        own_rows = lax.dynamic_slice_in_dim(full_term, offset, rows_dev, 1)
        result = result + own_rows.astype(jnp.float32)
    return (result, force_bias)


def solution(mesh):
    return jax.shard_map(
        shards,
        mesh=mesh,
        in_specs=(
            P("blk", "rows", None),
            P("blk", "rows", None),
            P(None, "blk"),
            P("blk", "rows", None),
        ),
        out_specs=(P("blk", "rows", None), P(None, "blk")),
        check_vma=False,
    )
```

profile of v0, /device:TPU:0, one launch (start us, length us, event | category | flops | bytes accessed | tf_op | source)
XLA Modules:
  0.0 360.4 jit_solution(13983244792735845269)
XLA Ops:
  7.2 0.0 all-gather.4.cloned.1.call-start
  7.2 2.8 copy.6
  10.0 0.0 all-gather.4.cloned.1.call-update
  10.0 0.0 all-reduce.2.cloned.1.call-start
  10.1 57.4 %all-gather.4.cloned.1.call-done = bf16[256,64,256]{2,0,1:T(8,128)(2,1)} async-done(((bf16[32,64,256]{2,0,1:T(8,128)(2,1)}), bf16[256,64,256]{2,0,1:T(8,128)(2,1)}) %all-gather.4.cloned.1.call-update) | async-done | bytes 8388624 | tf_op jit(solution)/shard_map/all_gather | solution.py:14
  67.5 27.3 %fusion.5 = bf16[256,512]{1,0:T(8,128)(2,1)} fusion(bf16[256,64,256]{2,0,1:T(8,128)(2,1)} %all-gather.4.cloned.1.call-done, bf16[512,64,256]{2,1,0:T(8,128)(2,1)} %param.4), kind=kOutput, calls=%fused_computation.7 | convolution fusion | flops 4295098368 | bytes 25427968 | tf_op jit(solution)/shard_map/dot_general | solution.py:16
  94.7 0.0 reduce-scatter.2.cloned.1.call-start
  94.8 17.9 %copy.8 = bf16[64,8,64,256]{3,1,2,0:T(8,128)(2,1)} copy(bf16[64,8,64,256]{3,2,1,0:T(8,128)(2,1)} %bitcast.19) | data formatting | bytes 33554432
  112.7 17.8 %all-reduce.2.cloned.1.call-done = bf16[256,512]{1,0:T(8,128)(2,1)} async-done(((bf16[256,512]{1,0:T(8,128)(2,1)}), bf16[256,512]{1,0:T(8,128)(2,1)}) %all-reduce.2.cloned.1.call-update) | async-done | bytes 262160 | tf_op jit(solution)/shard_map/psum | solution.py:19
  130.5 1.0 convert_element_type.41
  131.5 12.7 %convolution_convert_fusion = bf16[256,16384]{1,0:T(8,128)(2,1)} fusion(bf16[512,16384]{1,0:T(8,128)(2,1)} %bitcast.18, f32[256,512]{1,0:T(8,128)S(1)} %copy-done.3, f32[256,512]{1,0:T(8,128)S(1)} %convert_element_type.41), kind=kOutput, calls=%fused_computation | convolution fusion | flops 4299554816 | bytes 26214400 | tf_op jit(solution)/shard_map/dot_general | solution.py:22
  144.2 0.0 reduce-scatter.2.cloned.1.call-update
  144.2 0.0 all-gather.8.cloned.1.call-start
  144.3 0.5 all-gather.8.cloned.1.call-update
  144.8 0.3 all-gather.6.cloned.1.call-start
  145.1 70.7 %reduce-scatter.2.cloned.1.call-done = bf16[32,16384]{1,0:T(8,128)(2,1)} async-done(((bf16[256,16384]{1,0:T(8,128)(2,1)}), bf16[32,16384]{1,0:T(8,128)(2,1)}) %reduce-scatter.2.cloned.1.call-update) | async-done | bytes 1048592 | tf_op jit(solution)/shard_map/reduce_scatter | solution.py:21
  215.7 2.4 copy.9
  218.2 44.7 %all-gather.8.cloned.1.call-done = bf16[32,256,128]{2,1,0:T(8,128)(2,1)} async-done(((bf16[32,64,128]{2,1,0:T(8,128)(2,1)}), bf16[32,256,128]{2,1,0:T(8,128)(2,1)}) %all-gather.8.cloned.1.call-update) | async-done | bytes 2097168 | tf_op jit(solution)/shard_map/all_gather | solution.py:30
  262.9 81.6 %all-gather.6.cloned.1.call-done = bf16[32,256,256]{2,1,0:T(8,128)(2,1)} async-done(((bf16[32,64,256]{2,1,0:T(8,128)(2,1)}), bf16[32,256,256]{2,1,0:T(8,128)(2,1)}) %all-gather.6.cloned.1.call-update) | async-done | bytes 4194320 | tf_op jit(solution)/shard_map/all_gather | solution.py:29
  344.4 4.2 %convolution_convert_fusion.1 = bf16[32,256,128]{2,1,0:T(8,128)(2,1)S(1)} fusion(bf16[32,256,256]{2,1,0:T(8,128)(2,1)} %all-gather.6.cloned.1.call-done, bf16[32,256,128]{2,1,0:T(8,128)(2,1)} %all-gather.8.cloned.1.call-done), kind=kOutput, calls=%fused_computation.5 | convolution fusion | flops 537919488 | bytes 8388608 | tf_op jit(solution)/shard_map/wik,wka->wia/dot_general | solution.py:33
  348.7 1.2 multiply_convert_fusion.1
  349.9 1.2 multiply_convert_fusion
  351.2 1.2 fusion.11
  352.5 1.4 convert_add_fusion
  (10 shorter events, 0.1 us)
Async XLA Ops:
  7.2 60.3 %all-gather.4.cloned.1.call-start = ((), (), s32[]{:S(2)}) async-start(), calls=%async_computation.1 | async-start | bytes 9437184 | tf_op jit(solution)/shard_map/all_gather | solution.py:14
  10.0 120.5 %all-reduce.2.cloned.1.call-start = ((), (), s32[]{:S(2)}) async-start(), calls=%async_computation.2 | async-start | bytes 524288 | tf_op jit(solution)/shard_map/psum | solution.py:19
  94.7 121.0 %reduce-scatter.2.cloned.1.call-start = ((), (), s32[]{:S(2)}) async-start(), calls=%async_computation.3 | async-start | bytes 9437184 | tf_op jit(solution)/shard_map/reduce_scatter | solution.py:21
  94.8 36.7 %copy-start.3 = (f32[256,512]{1,0:T(8,128)S(1)}, f32[256,512]{1,0:T(8,128)}, u32[]{:S(2)}) copy-start(f32[256,512]{1,0:T(8,128)} %param.6) | copy-start | bytes 1572868
  131.5 12.7 %copy-start.2 = (f32[256,512]{1,0:T(8,128)}, f32[256,512]{1,0:T(8,128)S(1)}, u32[]{:S(2)}) copy-start(f32[256,512]{1,0:T(8,128)S(1)} %convert_element_type.41) | copy-start | bytes 1572868
  144.2 118.7 %all-gather.8.cloned.1.call-start = ((), (), s32[]{:S(2)}) async-start(), calls=%async_computation.5 | async-start | bytes 2621440 | tf_op jit(solution)/shard_map/all_gather | solution.py:30
  144.8 199.6 %all-gather.6.cloned.1.call-start = ((), (), s32[]{:S(2)}) async-start(), calls=%async_computation.4 | async-start | bytes 5242880 | tf_op jit(solution)/shard_map/all_gather | solution.py:29
  344.4 4.3 %copy-start = (bf16[32,256,256]{2,1,0:T(8,128)(2,1)S(1)}, bf16[32,256,256]{2,1,0:T(8,128)(2,1)}, u32[]{:S(2)}) copy-start(bf16[32,256,256]{2,1,0:T(8,128)(2,1)} %all-gather.6.cloned.1.call-done) | copy-start | bytes 12582916
  351.2 1.3 copy-start.1
Sparse Core Ops, SparseCore 0:
  10.4 56.9 all-gather.3
  94.9 35.5 all-reduce.1
  144.3 71.3 reduce-scatter.1
  217.2 45.6 all-gather.7
  264.9 79.5 all-gather.5
where the time goes:
time: 361 us; the launch traced here: 360 us
  waiting for transfers between devices  273 us (76%)
  matrix products  47.9 us (13%)
  local copies, waits for them, and re-layouts  23.1 us (6%)
  between operations  13.9 us (4%)
    all_gather x1, waiting for transfers between devices, shards(): full_potential = lax.all_gather(potential, 'rows', axis=1, tiled=True)  81.6 us
    reduce_scatter x1, waiting for transfers between devices, shards(): lax.psum_scatter(jnp.dot(shifted, flat_chol, preferred_element_type=jnp.f...  70.7 us
    all_gather x1, waiting for transfers between devices, shards(): batch_piece = lax.all_gather(green, 'blk', axis=0, tiled=True)  57.4 us
    all_gather x1, waiting for transfers between devices, shards(): full_term = lax.all_gather(walker_orbitals, 'rows', axis=1, tiled=True)  44.7 us
    dot_general x1, matrix products, shards(): lax.dot_general(flat_piece, flat_chol, (((1,), (1,)), ((), ())), preferre...  27.3 us
    unnamed x11, local copies, waits for them, and re-layouts  23.1 us
    psum x1, waiting for transfers between devices, shards(): lax.psum(partial_bias.astype(jnp.bfloat16), 'rows').astype(jnp.float32)  17.8 us
    dot_general x1, matrix products, shards(): jnp.dot(shifted, flat_chol, preferred_element_type=jnp.float32)  12.7 us
  transfers between devices with their start and end apart: 5, of which 5 were waited for; matrix products, arithmetic and copies ran while one was open for 6% of the time, Pallas kernels for 0%

commit v1 on v0

--- a/solution.py
+++ b/solution.py
@@ -27,7 +27,18 @@
     potential = summed.reshape(walk_count, rows_dev, orbitals)
     result = walker_orbitals.astype(jnp.float32)
     full_potential = lax.all_gather(potential, "rows", axis=1, tiled=True)
-    full_term = lax.all_gather(walker_orbitals, "rows", axis=1, tiled=True)
+    sheet = walker_orbitals
+    even = lax.psum(1, "rows")
+    e_next = lax.axis_index("rows")
+    near, fresh, back = (even, e_next, sheet.shape[1])
+    ledger = [dev_j * near if q == 1 else dev_j for q, dev_j in enumerate(sheet.shape)]
+    parts_out = jnp.zeros(ledger, sheet.dtype)
+    full_term = lax.dynamic_update_slice_in_dim(parts_out, sheet, fresh * back, axis=1)
+    for src_i in range(1, near):
+        sheet = lax.ppermute(sheet, "rows", [(q, (q + 1) % near) for q in range(near)])
+        full_term = lax.dynamic_update_slice_in_dim(
+            full_term, sheet, (fresh - src_i) % near * back, axis=1
+        )
     offset = lax.axis_index("rows") * rows_dev
     for degree in range(1, TAYLOR + 1):
         product = jnp.einsum(

time: 361 us -> 340 us (0.942)
  waiting for transfers between devices: 273 us -> 230 us
  starting transfers between devices: 0.42 us -> 20.2 us
    ppermute x0 -> x3, waiting for transfers between devices: none -> 63.1 us  [shards(): lax.ppermute(sheet, 'rows', [(q, (q + 1) % near) for q in range(near)])]
    all_gather x1, waiting for transfers between devices: 81.6 us -> 19.8 us  [shards(): full_potential = lax.all_gather(potential, 'rows', axis=1, tiled=True)]
    all_gather x1 -> x0, waiting for transfers between devices: 44.7 us -> none  [shards(): full_term = lax.all_gather(walker_orbitals, 'rows', axis=1, tiled=True)]
    ppermute x0 -> x3, starting transfers between devices: none -> 20 us  [shards(): lax.ppermute(sheet, 'rows', [(q, (q + 1) % near) for q in range(near)])]
  transfers between devices with their start and end apart: 5 -> 7, of which waited for: 5 -> 7; matrix products, arithmetic and copies ran while one was open for 6% -> 6% of each run, Pallas kernels for 0% -> 0%
where the time goes in v1:
time: 340 us; the launch traced here: 339 us
  waiting for transfers between devices  230 us (68%)
  matrix products  47.2 us (14%)
  local copies, waits for them, and re-layouts  26 us (8%)
  starting transfers between devices  20.2 us (6%)
  between operations  13.9 us (4%)
    reduce_scatter x1, waiting for transfers between devices, shards(): lax.psum_scatter(jnp.dot(shifted, flat_chol, preferred_element_type=jnp.f...  71.5 us
    ppermute x3, waiting for transfers between devices, shards(): lax.ppermute(sheet, 'rows', [(q, (q + 1) % near) for q in range(near)])  63.1 us
    all_gather x1, waiting for transfers between devices, shards(): batch_piece = lax.all_gather(green, 'blk', axis=0, tiled=True)  57.4 us
    dot_general x1, matrix products, shards(): lax.dot_general(flat_piece, flat_chol, (((1,), (1,)), ((), ())), preferre...  27.3 us
    unnamed x11, local copies, waits for them, and re-layouts  23.1 us
    ppermute x3, starting transfers between devices, shards(): lax.ppermute(sheet, 'rows', [(q, (q + 1) % near) for q in range(near)])  20 us
    all_gather x1, waiting for transfers between devices, shards(): full_potential = lax.all_gather(potential, 'rows', axis=1, tiled=True)  19.8 us
    psum x1, waiting for transfers between devices, shards(): lax.psum(partial_bias.astype(jnp.bfloat16), 'rows').astype(jnp.float32)  17.8 us
  transfers between devices with their start and end apart: 7, of which 7 were waited for; matrix products, arithmetic and copies ran while one was open for 6% of the time, Pallas kernels for 0%

profile of v1, /device:TPU:0, one launch (start us, length us, event | category | flops | bytes accessed | tf_op | source)
XLA Modules:
  0.0 339.3 jit_solution(7790552067748670331)
XLA Ops:
  7.2 2.8 copy.6
  10.1 57.4 %all-gather.3.cloned.1.call-done = bf16[256,64,256]{2,0,1:T(8,128)(2,1)} async-done(((bf16[32,64,256]{2,0,1:T(8,128)(2,1)}), bf16[256,64,256]{2,0,1:T(8,128)(2,1)}) %all-gather.3.cloned.1.call-update) | async-done | bytes 8388624 | tf_op jit(solution)/shard_map/all_gather | solution.py:14
  67.5 27.3 %fusion.5 = bf16[256,512]{1,0:T(8,128)(2,1)} fusion(bf16[256,64,256]{2,0,1:T(8,128)(2,1)} %all-gather.3.cloned.1.call-done, bf16[512,64,256]{2,1,0:T(8,128)(2,1)} %param.4), kind=kOutput, calls=%fused_computation.7 | convolution fusion | flops 4295098368 | bytes 25427968 | tf_op jit(solution)/shard_map/dot_general | solution.py:16
  94.8 17.9 %copy.8 = bf16[64,8,64,256]{3,1,2,0:T(8,128)(2,1)} copy(bf16[64,8,64,256]{3,2,1,0:T(8,128)(2,1)} %bitcast.19) | data formatting | bytes 33554432
  112.7 17.8 %all-reduce.2.cloned.1.call-done = bf16[256,512]{1,0:T(8,128)(2,1)} async-done(((bf16[256,512]{1,0:T(8,128)(2,1)}), bf16[256,512]{1,0:T(8,128)(2,1)}) %all-reduce.2.cloned.1.call-update) | async-done | bytes 262160 | tf_op jit(solution)/shard_map/psum | solution.py:19
  130.5 1.0 convert_element_type.41
  131.5 12.7 %convolution_convert_fusion = bf16[256,16384]{1,0:T(8,128)(2,1)} fusion(bf16[512,16384]{1,0:T(8,128)(2,1)} %bitcast.18, f32[256,512]{1,0:T(8,128)S(1)} %copy-done.3, f32[256,512]{1,0:T(8,128)S(1)} %convert_element_type.41), kind=kOutput, calls=%fused_computation | convolution fusion | flops 4299554816 | bytes 26214400 | tf_op jit(solution)/shard_map/dot_general | solution.py:22
  144.3 71.5 %reduce-scatter.2.cloned.1.call-done = bf16[32,16384]{1,0:T(8,128)(2,1)} async-done(((bf16[256,16384]{1,0:T(8,128)(2,1)}), bf16[32,16384]{1,0:T(8,128)(2,1)}) %reduce-scatter.2.cloned.1.call-update) | async-done | bytes 1048592 | tf_op jit(solution)/shard_map/reduce_scatter | solution.py:21
  215.7 2.4 copy.9
  218.2 1.5 collective-permute-start
  219.8 17.6 %collective-permute-done = bf16[32,64,128]{2,1,0:T(8,128)(2,1)S(1)} collective-permute-done((bf16[32,64,128]{2,1,0:T(8,128)(2,1)S(1)}, bf16[32,64,128]{2,1,0:T(8,128)(2,1)S(1)}, u32[]{:S(2)}, u32[]{:S(2)}) %collective-permute-start) | collective-permute-done | bytes 524320 | tf_op jit(solution)/shard_map/ppermute | solution.py:38
  237.3 4.9 %collective-permute-start.1 = (bf16[32,64,128]{2,1,0:T(8,128)(2,1)S(1)}, bf16[32,64,128]{2,1,0:T(8,128)(2,1)}, u32[]{:S(2)}, u32[]{:S(2)}) collective-permute-start(bf16[32,64,128]{2,1,0:T(8,128)(2,1)S(1)} %collective-permute-done), channel_id=1, source_target_pairs={{0,1},{1,2},{2,3},{3,0},{4,5},{5,6},{6,7},{7,4},{8,9},{9,10},{10,1... | collective-permute-start | bytes 1572872 | tf_op jit(solution)/shard_map/ppermute | solution.py:38
  242.2 23.9 %collective-permute-done.1 = bf16[32,64,128]{2,1,0:T(8,128)(2,1)} collective-permute-done((bf16[32,64,128]{2,1,0:T(8,128)(2,1)S(1)}, bf16[32,64,128]{2,1,0:T(8,128)(2,1)}, u32[]{:S(2)}, u32[]{:S(2)}) %collective-permute-start.1) | collective-permute-done | bytes 524320 | tf_op jit(solution)/shard_map/ppermute | solution.py:38
  266.1 13.6 %collective-permute-start.2 = (bf16[32,64,128]{2,1,0:T(8,128)(2,1)}, bf16[32,64,128]{2,1,0:T(8,128)(2,1)}, u32[]{:S(2)}, u32[]{:S(2)}) collective-permute-start(bf16[32,64,128]{2,1,0:T(8,128)(2,1)} %collective-permute-done.1), channel_id=1, source_target_pairs={{0,1},{1,2},{2,3},{3,0},{4,5},{5,6},{6,7},{7,4},{8,9},{9,10},{10,1... | collective-permute-start | bytes 1572872 | tf_op jit(solution)/shard_map/ppermute | solution.py:38
  279.7 0.5 broadcast_in_dim.3
  280.4 1.1 constant_dynamic-update-slice_fusion.1
  281.5 21.6 %collective-permute-done.2 = bf16[32,64,128]{2,1,0:T(8,128)(2,1)} collective-permute-done((bf16[32,64,128]{2,1,0:T(8,128)(2,1)}, bf16[32,64,128]{2,1,0:T(8,128)(2,1)}, u32[]{:S(2)}, u32[]{:S(2)}) %collective-permute-start.2) | collective-permute-done | bytes 524320 | tf_op jit(solution)/shard_map/ppermute | solution.py:38
  303.1 1.1 constant_dynamic-update-slice_fusion
  304.2 19.8 %all-gather.5.cloned.1.call-done = bf16[32,256,256]{2,1,0:T(8,128)(2,1)} async-done(((bf16[32,64,256]{2,1,0:T(8,128)(2,1)}), bf16[32,256,256]{2,1,0:T(8,128)(2,1)}) %all-gather.5.cloned.1.call-update) | async-done | bytes 4194320 | tf_op jit(solution)/shard_map/all_gather | solution.py:29
  324.1 3.6 %convolution_convert_fusion.1 = bf16[32,256,128]{2,1,0:T(8,128)(2,1)S(1)} fusion(bf16[32,256,256]{2,1,0:T(8,128)(2,1)} %all-gather.5.cloned.1.call-done, bf16[32,256,128]{2,1,0:T(8,128)(2,1)S(1)} %constant_dynamic-update-slice_fusion), kind=kOutput, calls=%fused_computation.5 | convolution fusion | flops 537919488 | bytes 8388608 | tf_op jit(solution)/shard_map/wik,wka->wia/dot_general | solution.py:44
  327.7 1.2 multiply_convert_fusion.1
  328.9 1.2 multiply_convert_fusion
  330.2 1.2 fusion.11
  331.4 1.4 convert_add_fusion
  (18 shorter events, 0.4 us)
Async XLA Ops:
  7.2 60.3 %all-gather.3.cloned.1.call-start = ((), (), s32[]{:S(2)}) async-start(), calls=%async_computation.1 | async-start | bytes 9437184 | tf_op jit(solution)/shard_map/all_gather | solution.py:14
  10.0 120.5 %all-reduce.2.cloned.1.call-start = ((), (), s32[]{:S(2)}) async-start(), calls=%async_computation.2 | async-start | bytes 524288 | tf_op jit(solution)/shard_map/psum | solution.py:19
  94.7 121.0 %reduce-scatter.2.cloned.1.call-start = ((), (), s32[]{:S(2)}) async-start(), calls=%async_computation.3 | async-start | bytes 9437184 | tf_op jit(solution)/shard_map/reduce_scatter | solution.py:21
  94.8 36.7 %copy-start.3 = (f32[256,512]{1,0:T(8,128)S(1)}, f32[256,512]{1,0:T(8,128)}, u32[]{:S(2)}) copy-start(f32[256,512]{1,0:T(8,128)} %param.6) | copy-start | bytes 1572868
  131.5 12.7 %copy-start.1 = (f32[256,512]{1,0:T(8,128)}, f32[256,512]{1,0:T(8,128)S(1)}, u32[]{:S(2)}) copy-start(f32[256,512]{1,0:T(8,128)S(1)} %convert_element_type.41) | copy-start | bytes 1572868
  144.2 74.0 %copy-start.2 = (bf16[32,64,128]{2,1,0:T(8,128)(2,1)S(1)}, bf16[32,64,128]{2,1,0:T(8,128)(2,1)}, u32[]{:S(2)}) copy-start(bf16[32,64,128]{2,1,0:T(8,128)(2,1)} %param.7) | copy-start | bytes 1572868
  144.2 179.9 %all-gather.5.cloned.1.call-start = ((), (), s32[]{:S(2)}) async-start(), calls=%async_computation.4 | async-start | bytes 5242880 | tf_op jit(solution)/shard_map/all_gather | solution.py:29
  218.2 19.1 %collective-permute-start = (bf16[32,64,128]{2,1,0:T(8,128)(2,1)S(1)}, bf16[32,64,128]{2,1,0:T(8,128)(2,1)S(1)}, u32[]{:S(2)}, u32[]{:S(2)}) collective-permute-start(bf16[32,64,128]{2,1,0:T(8,128)(2,1)S(1)} %copy-done.2), channel_id=1, source_target_pairs={{0,1},{1,2},{2,3},{3,0},{4,5},{5,6},{6,7},{7,4},{8,9},{9,10},{10,1... | collective-permute-start | bytes 1572872 | tf_op jit(solution)/shard_map/ppermute | solution.py:38
  237.3 28.8 %collective-permute-start.1 = (bf16[32,64,128]{2,1,0:T(8,128)(2,1)S(1)}, bf16[32,64,128]{2,1,0:T(8,128)(2,1)}, u32[]{:S(2)}, u32[]{:S(2)}) collective-permute-start(bf16[32,64,128]{2,1,0:T(8,128)(2,1)S(1)} %collective-permute-done), channel_id=1, source_target_pairs={{0,1},{1,2},{2,3},{3,0},{4,5},{5,6},{6,7},{7,4},{8,9},{9,10},{10,1... | collective-permute-start | bytes 1572872 | tf_op jit(solution)/shard_map/ppermute | solution.py:38
  266.1 37.0 %collective-permute-start.2 = (bf16[32,64,128]{2,1,0:T(8,128)(2,1)}, bf16[32,64,128]{2,1,0:T(8,128)(2,1)}, u32[]{:S(2)}, u32[]{:S(2)}) collective-permute-start(bf16[32,64,128]{2,1,0:T(8,128)(2,1)} %collective-permute-done.1), channel_id=1, source_target_pairs={{0,1},{1,2},{2,3},{3,0},{4,5},{5,6},{6,7},{7,4},{8,9},{9,10},{10,1... | collective-permute-start | bytes 1572872 | tf_op jit(solution)/shard_map/ppermute | solution.py:38
  324.1 3.6 %copy-start = (bf16[32,256,256]{2,1,0:T(8,128)(2,1)S(1)}, bf16[32,256,256]{2,1,0:T(8,128)(2,1)}, u32[]{:S(2)}) copy-start(bf16[32,256,256]{2,1,0:T(8,128)(2,1)} %all-gather.5.cloned.1.call-done) | copy-start | bytes 12582916
Sparse Core Ops, SparseCore 0:
  10.4 56.9 all-gather.2
  94.9 35.5 all-reduce.1
  144.3 71.3 reduce-scatter.1
  218.3 105.6 all-gather.4
